TPU v7x, 32 devices: a whole 2x2x4 slice. The times are simulated.
32 devices in a mesh: dp: 8 (over y, x, core), mp: 4 (over z).
Axes of the slice: x: 2, y: 2, z: 4, core: 2. Of those that a mesh axis runs over, the one named last changes fastest.
Arguments:
- hidden_states: bfloat16 [4096, 4096], P('dp', 'mp'), may hold values from -40 to 40
- norm_gain: float32 [1, 4096], replicated, may hold values from 0.1 to 1.9
- query_weight: bfloat16 [1, 4096, 4096], P(None, 'dp', 'mp'), may hold values from -0.01171875 to 0.01171875
- keyvalue_weight: bfloat16 [1, 4096, 2, 4096], P(None, 'dp', None, 'mp'), may hold values from -0.09375 to 0.09375
- output_weight: bfloat16 [1, 4096, 4096], P(None, 'dp', 'mp'), may hold values from -0.09375 to 0.09375
- position_bias: float32 [1, 32, 64], P(None, None, 'mp'), may hold values from -8 to 250
- lengths: int32 [32], P('dp'), may hold values from 16 to 128
Outputs:
- layer_output: bfloat16 [4096, 4096], P('dp', 'mp')
All inputs are finite; a program needn't handle non-finite values.
Results may differ from a plain program's by a relative error of at most 0.006.
Values may be sent and summed in bfloat16 or wider, within the bound.
No kernel may reach another device: no remote copies, remote signals or barrier semaphores. Data moves between devices by JAX's collectives and lax.ppermute only.
A program may use at most 128 MiB of HBM per device.

v0:
```python
import jax
import jax.numpy as jnp
import numpy as np
from jax import lax
from jax.sharding import PartitionSpec as P

DH = 64
BUCKETS = 32
DIST = 128
LEN = 128
epsilon = 1e-06


def bucket_table():
    half_count = BUCKETS // 2
    exact_count = half_count // 2
    positions = np.arange(LEN)
    relative = positions[None, :] - positions[:, None]
    distance = np.abs(relative)
    scaled = (
        np.log(np.maximum(distance, 1) / exact_count)
        / np.log(DIST / exact_count)
        * (half_count - exact_count)
    )
    far_bucket = np.minimum(exact_count + np.floor(scaled + 1e-09).astype(np.int32), half_count - 1)
    near_bucket = np.where(distance < exact_count, distance, far_bucket)
    return (near_bucket + np.where(relative > 0, half_count, 0)).astype(np.int32)


def normed_rows(hidden, gain_row):
    values = hidden.astype(jnp.float32)
    mean_square = jnp.mean(values * values, axis=-1, keepdims=True)
    return (values * lax.rsqrt(mean_square + epsilon) * gain_row).astype(jnp.bfloat16)


def add_projections(query_acc, pair_acc, normed, query_piece, pair_piece):
    query_acc = jnp.dot(normed, query_piece, preferred_element_type=jnp.float32)
    pair_acc = jnp.einsum("td,dcf->ctf", normed, pair_piece, preferred_element_type=jnp.float32)
    return (query_acc, pair_acc)


def local(
    hidden_states, norm_gain, query_weight, keyvalue_weight, output_weight, position_bias, lengths
):
    captions = lengths.shape[0]
    tokens_here = hidden_states.shape[0]
    heads_here = position_bias.shape[2]
    inner_here = heads_here * DH
    bucket_onehot = jnp.asarray(
        (bucket_table()[:, :, None] == np.arange(BUCKETS)[None, None, :]).astype(np.float32)
    )
    visible = jnp.arange(LEN)[None, :] < lengths[:, None]
    hidden = hidden_states
    gathered = lax.all_gather(hidden, "mp", axis=1, tiled=True)
    normed = normed_rows(gathered, norm_gain[0])
    zero_queries = jnp.zeros((tokens_here, inner_here), jnp.float32)
    zero_pairs = jnp.zeros((2, tokens_here, inner_here), jnp.float32)
    query_rows = query_weight[0]
    pair_rows = keyvalue_weight[0]
    out_rows = output_weight[0]
    query_acc, pair_acc = add_projections(
        zero_queries,
        zero_pairs,
        normed,
        lax.all_gather(query_rows, "dp", axis=0, tiled=True),
        lax.all_gather(pair_rows, "dp", axis=0, tiled=True),
    )
    queries = query_acc.astype(jnp.bfloat16).reshape(captions, LEN, heads_here, DH)
    key_rows = pair_acc[0].astype(jnp.bfloat16).reshape(captions, LEN, heads_here, DH)
    value_rows = pair_acc[1].astype(jnp.bfloat16).reshape(captions, LEN, heads_here, DH)
    position_terms = jnp.einsum(
        "qkb,bh->hqk", bucket_onehot, position_bias[0], precision=lax.Precision.HIGHEST
    )
    scores = (
        jnp.einsum("cqhe,ckhe->chqk", queries, key_rows, preferred_element_type=jnp.float32)
        + position_terms[None]
    )
    scores = jnp.where(visible[:, None, None, :], scores, -1e30)
    maxima = jnp.max(scores, axis=-1, keepdims=True)
    raised = jnp.exp(scores - maxima)
    weights = (raised / jnp.sum(raised, axis=-1, keepdims=True)).astype(jnp.bfloat16)
    mixture = jnp.einsum("chqk,ckhe->cqhe", weights, value_rows, preferred_element_type=jnp.float32)
    attended = mixture.astype(jnp.bfloat16).reshape(tokens_here, inner_here)
    partial_out = jnp.einsum(
        "tf,df->td",
        attended,
        lax.all_gather(out_rows, "dp", axis=0, tiled=True),
        preferred_element_type=jnp.float32,
    )
    reduced = lax.psum_scatter(
        partial_out.astype(jnp.bfloat16), "mp", scatter_dimension=1, tiled=True
    ).astype(jnp.float32)
    hidden = (hidden.astype(jnp.float32) + reduced).astype(jnp.bfloat16)
    return hidden


def solution(mesh):
    in_specs = (
        P("dp", "mp"),
        P(),
        P(None, "dp", "mp"),
        P(None, "dp", None, "mp"),
        P(None, "dp", "mp"),
        P(None, None, "mp"),
        P("dp"),
    )
    out_specs = P("dp", "mp")
    return jax.shard_map(local, mesh=mesh, in_specs=in_specs, out_specs=out_specs, check_vma=False)
```

profile of v0, /device:TPU:0, one launch (start us, length us, event | category | flops | bytes accessed | tf_op | source)
XLA Modules:
  0.0 390.5 jit_solution(6013965719425897973)
XLA Ops:
  6.5 0.0 copy-start
  6.5 0.0 all-gather.8.cloned.1.call-start
  6.5 0.7 all-gather.8.cloned.1.call-update
  7.3 0.0 copy-start.3
  7.3 0.0 all-gather.12.cloned.1.call-start
  7.3 0.7 all-gather.12.cloned.1.call-update
  8.0 0.0 all-gather.10.cloned.1.call-start
  8.1 3.5 copy.15
  11.6 0.0 copy-start.7
  11.6 0.0 all-gather.10.cloned.1.call-update
  11.6 0.0 all-gather.14.cloned.1.call-start
  11.7 0.5 all-gather.14.cloned.1.call-update
  12.2 0.0 copy-start.6
  12.2 0.0 reduce-scatter.2.cloned.1.call-start
  12.3 0.0 copy-done
  12.3 0.0 copy-done.3
  12.3 1.2 convolution_bitcast_fusion
  13.5 1.4 copy.21
  14.9 0.0 copy-done.7
  14.9 0.1 iota_compare_fusion
  15.0 77.4 %all-gather.8.cloned.1.call-done = bf16[512,4096]{1,0:T(8,128)(2,1)} async-done(((bf16[512,1024]{1,0:T(8,128)(2,1)}), bf16[512,4096]{1,0:T(8,128)(2,1)}) %all-gather.8.cloned.1.call-update) | async-done | bytes 4194320 | tf_op jit(solution)/shard_map/all_gather | solution.py:54
  92.4 3.1 fusion.3
  95.5 51.6 %all-gather.12.cloned.1.call-done = bf16[1,4096,1024]{2,1,0:T(8,128)(2,1)} async-done(((bf16[1,512,1024]{2,1,0:T(8,128)(2,1)}), bf16[1,4096,1024]{2,1,0:T(8,128)(2,1)}) %all-gather.12.cloned.1.call-update) | async-done | bytes 8388624 | tf_op jit(solution)/shard_map/all_gather | solution.py:65
  147.1 0.0 copy-done.6
  147.1 9.2 %fusion.27 = bf16[512,1024]{1,0:T(8,128)(2,1)S(1)} fusion(bf16[1,4096,1024]{2,1,0:T(8,128)(2,1)} %all-gather.12.cloned.1.call-done, bf16[512,4096]{1,0:T(8,128)(2,1)} %all-gather.8.cloned.1.call-done, f32[4096]{0:T(1024)S(1)} %bitcast.40, f32[512]{0:T(512)S(1)} %add_rsqrt_fusion), kind=kOutput, calls=%fused_computation.28 | convolution fusion | flops 4303880192 | bytes 13649920 | tf_op jit(solution)/shard_map/dot_general | solution.py:37
  156.3 1.5 reshape.48
  157.8 80.9 %all-gather.10.cloned.1.call-done = bf16[1,4096,2,1024]{3,1,2,0:T(8,128)(2,1)} async-done(((bf16[1,512,2,1024]{3,1,2,0:T(8,128)(2,1)}), bf16[1,4096,2,1024]{3,1,2,0:T(8,128)(2,1)}) %all-gather.10.cloned.1.call-update) | async-done | bytes 16777232 | tf_op jit(solution)/shard_map/all_gather | solution.py:66
  238.7 13.7 %convert_bitcast_fusion = bf16[2,512,1024]{2,1,0:T(8,128)(2,1)S(1)} fusion(bf16[1,4096,2,1024]{3,1,2,0:T(8,128)(2,1)} %all-gather.10.cloned.1.call-done, bf16[512,4096]{1,0:T(8,128)(2,1)} %all-gather.8.cloned.1.call-done, f32[4096]{0:T(1024)S(1)} %bitcast.41, f32[512]{0:T(512)S(1)} %add_rsqrt_fusion), kind=kOutput, calls=%fused_computation.23 | convolution fusion | flops 8599371776 | bytes 23087104 | tf_op jit(solution)/shard_map/td,dcf->ctf/dot_general | solution.py:38
  252.4 1.1 fusion.42
  253.6 4.0 %reshape.49 = bf16[4,128,16,64]{3,2,1,0:T(8,128)(2,1)} reshape(bf16[1,512,1024]{2,1,0:T(8,128)(2,1)} %get-tuple-element.6) | data formatting | bytes 2097152 | tf_op jit(solution)/shard_map/convert_element_type | solution.py:69
  257.6 2.3 reshape.47
  259.9 0.0 copy-start.5
  259.9 3.3 fusion.15
  263.2 0.0 copy-done.5
  263.2 0.0 copy-start.4
  263.2 1.8 fusion.43
  265.0 0.0 copy-done.4
  265.0 0.8 fusion.33
  265.8 0.9 copy.24
  266.7 28.1 %all-gather.14.cloned.1.call-done = bf16[1,4096,1024]{2,1,0:T(8,128)(2,1)} async-done(((bf16[1,512,1024]{2,1,0:T(8,128)(2,1)}), bf16[1,4096,1024]{2,1,0:T(8,128)(2,1)}) %all-gather.14.cloned.1.call-update) | async-done | bytes 8388624 | tf_op jit(solution)/shard_map/all_gather | solution.py:87
  294.8 0.0 copy-start.1
  294.8 9.6 %fusion.10 = bf16[512,4096]{1,0:T(8,128)(2,1)} fusion(bf16[1,4096,1024]{2,1,0:T(8,128)(2,1)} %all-gather.14.cloned.1.call-done, bf16[128,8,4,128]{3,2,1,0:T(4,128)(2,1)S(1)} %bitcast.39), kind=kOutput, calls=%fused_computation.12 | convolution fusion | flops 4297064448 | bytes 13631488 | tf_op jit(solution)/shard_map/tf,df->td/dot_general | solution.py:84
  304.4 0.0 copy-start.2
  304.4 0.0 reduce-scatter.2.cloned.1.call-update
  304.4 77.0 %reduce-scatter.2.cloned.1.call-done = bf16[512,1024]{1,0:T(8,128)(2,1)} async-done(((bf16[512,4096]{1,0:T(8,128)(2,1)}), bf16[512,1024]{1,0:T(8,128)(2,1)}) %reduce-scatter.2.cloned.1.call-update) | async-done | bytes 1048592 | tf_op jit(solution)/shard_map/reduce_scatter | solution.py:90
  381.3 0.0 copy-done.2
  381.3 2.6 add_convert_fusion
  383.9 0.0 copy-done.1
  (1 shorter events, 0.0 us)
Async XLA Ops:
  6.5 5.7 %copy-start = (f32[1,32,16]{1,2,0:T(8,128)S(1)}, f32[1,32,16]{1,2,0:T(8,128)}, u32[]{:S(2)}) copy-start(f32[1,32,16]{1,2,0:T(8,128)} %param.13) | copy-start | bytes 6148
  6.5 85.9 %all-gather.8.cloned.1.call-start = ((), (), s32[]{:S(2)}) async-start(), calls=%async_computation.1 | async-start | bytes 5242880 | tf_op jit(solution)/shard_map/all_gather | solution.py:54
  7.3 5.0 %copy-start.3 = (f32[128,128,32]{1,2,0:T(8,128)S(1)}, f32[128,128,32]{1,2,0:T(8,128)}, u32[]{:S(2)}) copy-start(f32[128,128,32]{1,2,0:T(8,128)} %constant.13.clone) | copy-start | bytes 6291460
  7.3 139.8 %all-gather.12.cloned.1.call-start = ((), (), s32[]{:S(2)}) async-start(), calls=%async_computation.4 | async-start | bytes 9437184 | tf_op jit(solution)/shard_map/all_gather | solution.py:65
  8.0 230.7 %all-gather.10.cloned.1.call-start = ((), (), s32[]{:S(2)}) async-start(), calls=%async_computation.3 | async-start | bytes 18874368 | tf_op jit(solution)/shard_map/all_gather | solution.py:66
  11.6 3.3 copy-start.7
  11.6 283.2 %all-gather.14.cloned.1.call-start = ((), (), s32[]{:S(2)}) async-start(), calls=%async_computation.5 | async-start | bytes 9437184 | tf_op jit(solution)/shard_map/all_gather | solution.py:87
  12.2 134.9 %copy-start.6 = (f32[1,4096]{1,0:T(1,128)S(1)}, f32[1,4096]{1,0:T(1,128)}, u32[]{:S(2)}) copy-start(f32[1,4096]{1,0:T(1,128)} %param.9) | copy-start | bytes 49156
  12.2 369.1 %reduce-scatter.2.cloned.1.call-start = ((), (), s32[]{:S(2)}) async-start(), calls=%async_computation.2 | async-start | bytes 5242880 | tf_op jit(solution)/shard_map/reduce_scatter | solution.py:90
  259.9 3.3 copy-start.5
  263.2 1.8 copy-start.4
  294.8 89.2 %copy-start.1 = (f32[1,32,16]{1,2,0:T(8,128)S(1)}, f32[1,32,16]{1,2,0:T(8,128)}, u32[]{:S(2)}) copy-start(f32[1,32,16]{1,2,0:T(8,128)} %param.13) | copy-start | bytes 6148
  304.4 77.0 %copy-start.2 = (bf16[512,1024]{1,0:T(8,128)(2,1)S(1)}, bf16[512,1024]{1,0:T(8,128)(2,1)}, u32[]{:S(2)}) copy-start(bf16[512,1024]{1,0:T(8,128)(2,1)} %param.8) | copy-start | bytes 3145732
Sparse Core Ops, SparseCore 0:
  8.9 83.4 all-gather.7
  94.3 52.7 all-gather.11
  149.0 89.7 all-gather.9
  240.5 54.2 all-gather.13
  304.5 76.7 reduce-scatter.1
where the time goes:
time: 391 us; the launch traced here: 390 us
  waiting for transfers between devices  317 us (81%)
  matrix products  37.7 us (10%)
  local copies, waits for them, and re-layouts  14.9 us (4%)
  between operations  13.2 us (3%)
  other arithmetic  7.56 us (2%)
    all_gather x1, waiting for transfers between devices, local(): lax.all_gather(pair_rows, 'dp', axis=0, tiled=True)  80.9 us
    all_gather x1, waiting for transfers between devices, local(): gathered = lax.all_gather(hidden, 'mp', axis=1, tiled=True)  77.4 us
    reduce_scatter x1, waiting for transfers between devices, local(): lax.psum_scatter(partial_out.astype(jnp.bfloat16), 'mp', scatter_dimensio...  77 us
    all_gather x1, waiting for transfers between devices, local(): lax.all_gather(query_rows, 'dp', axis=0, tiled=True)  51.6 us
    all_gather x1, waiting for transfers between devices, local(): lax.all_gather(out_rows, 'dp', axis=0, tiled=True)  28.1 us
    dot_general x1, matrix products, add_projections(): jnp.einsum('td,dcf->ctf', normed, pair_piece, preferred_element_type=jnp....  13.7 us
    dot_general x1, matrix products, local(): jnp.einsum('tf,df->td', attended, lax.all_gather(out_rows, 'dp', axis=0,...  9.59 us
    dot_general x1, matrix products, add_projections(): query_acc = jnp.dot(normed, query_piece, preferred_element_type=jnp.float32)  9.19 us
  transfers between devices with their start and end apart: 5, of which 5 were waited for; matrix products, arithmetic and copies ran while one was open for 12% of the time, Pallas kernels for 0%

commit v1 on v0

--- a/solution.py
+++ b/solution.py
@@ -51,7 +51,23 @@
     )
     visible = jnp.arange(LEN)[None, :] < lengths[:, None]
     hidden = hidden_states
-    gathered = lax.all_gather(hidden, "mp", axis=1, tiled=True)
+
+    def produce_the_members_all(chunk, row_axis):
+        lanes = lax.axis_size(row_axis)
+        steps_seen = [chunk]
+        for src_i in [*range(lanes - 1)]:
+            steps_seen.append(
+                lax.ppermute(
+                    steps_seen[-1], row_axis, [(num, (num + 1) % lanes) for num in range(lanes)]
+                )
+            )
+        return jnp.roll(
+            jnp.concatenate(steps_seen[::-1], axis=1),
+            (lax.axis_index(row_axis) + 1) * chunk.shape[1],
+            1,
+        )
+
+    gathered = produce_the_members_all(hidden, "mp")
     normed = normed_rows(gathered, norm_gain[0])
     zero_queries = jnp.zeros((tokens_here, inner_here), jnp.float32)
     zero_pairs = jnp.zeros((2, tokens_here, inner_here), jnp.float32)

time: 391 us -> 310 us (0.79)
  waiting for transfers between devices: 317 us -> 220 us
  local copies, waits for them, and re-layouts: 14.9 us -> 27.1 us
    all_gather x1 -> x0, waiting for transfers between devices: 77.4 us -> none  [local(): gathered = lax.all_gather(hidden, 'mp', axis=1, tiled=True)]
    ppermute x0 -> x3, waiting for transfers between devices: none -> 72.7 us  [produce_the_members_all(): lax.ppermute(steps_seen[-1], row_axis, [(num, (num + 1) % lanes) for num...]
    all_gather x1, waiting for transfers between devices: 51.6 us -> 0.02 us  [local(): lax.all_gather(query_rows, 'dp', axis=0, tiled=True)]
    all_gather x1, waiting for transfers between devices: 80.9 us -> 43.1 us  [local(): lax.all_gather(pair_rows, 'dp', axis=0, tiled=True)]
    unnamed x17 -> x24, local copies, waits for them, and re-layouts: 3.56 us -> 12.3 us
  transfers between devices with their start and end apart: 5 -> 7, of which waited for: 5 -> 6; matrix products, arithmetic and copies ran while one was open for 12% -> 19% of each run, Pallas kernels for 0% -> 0%
where the time goes in v1:
time: 310 us
  waiting for transfers between devices  220 us (71%)
  matrix products  40.3 us (13%)
  local copies, waits for them, and re-layouts  27.1 us (9%)
  between operations  13.3 us (4%)
  other arithmetic  5.37 us (2%)
  starting transfers between devices  3.23 us (1%)
    reduce_scatter x1, waiting for transfers between devices, local(): lax.psum_scatter(partial_out.astype(jnp.bfloat16), 'mp', scatter_dimensio...  77 us
    ppermute x3, waiting for transfers between devices, produce_the_members_all(): lax.ppermute(steps_seen[-1], row_axis, [(num, (num + 1) % lanes) for num...  72.7 us
    all_gather x1, waiting for transfers between devices, local(): lax.all_gather(pair_rows, 'dp', axis=0, tiled=True)  43.1 us
    all_gather x1, waiting for transfers between devices, local(): lax.all_gather(out_rows, 'dp', axis=0, tiled=True)  26.2 us
    dot_general x1, matrix products, add_projections(): jnp.einsum('td,dcf->ctf', normed, pair_piece, preferred_element_type=jnp....  13.7 us
    unnamed x24, local copies, waits for them, and re-layouts  12.3 us
    dot_general x1, matrix products, add_projections(): query_acc = jnp.dot(normed, query_piece, preferred_element_type=jnp.float32)  10.2 us
    dot_general x1, matrix products, local(): jnp.einsum('tf,df->td', attended, lax.all_gather(out_rows, 'dp', axis=0,...  9.6 us
  transfers between devices with their start and end apart: 7, of which 6 were waited for; matrix products, arithmetic and copies ran while one was open for 19% of the time, Pallas kernels for 0%

profile of v1, /device:TPU:0, one launch (start us, length us, event | category | flops | bytes accessed | tf_op | source)
XLA Modules:
  0.0 309.8 jit_solution(5803321465712935805)
XLA Ops:
  6.5 0.0 copy-start
  6.5 0.0 copy-start.2
  6.5 0.0 all-gather.9.cloned.1.call-start
  6.5 0.7 all-gather.9.cloned.1.call-update
  7.3 0.0 all-gather.7.cloned.1.call-start
  7.3 3.6 %copy.15 = bf16[1,512,2,1024]{3,1,2,0:T(8,128)(2,1)} copy(bf16[1,512,2,1024]{3,2,1,0:T(2,128)(2,1)} %param.11) | data formatting | bytes 4194304 | tf_op args[3]
  10.9 0.0 copy-start.7
  10.9 0.0 all-gather.7.cloned.1.call-update
  10.9 0.0 all-gather.11.cloned.1.call-start
  11.0 0.7 all-gather.11.cloned.1.call-update
  11.7 0.0 reduce-scatter.2.cloned.1.call-start
  11.7 0.0 copy-done.2
  11.7 3.1 %collective-permute-start = (bf16[512,1024]{1,0:T(8,128)(2,1)S(1)}, bf16[512,1024]{1,0:T(8,128)(2,1)S(1)}, u32[]{:S(2)}, u32[]{:S(2)}) collective-permute-start(bf16[512,1024]{1,0:T(8,128)(2,1)S(1)} %copy-done.2), channel_id=1, source_target_pairs={{0,1},{1,2},{2,3},{3,0},{4,5},{5,6},{6,7},{7,4},{8,9},{9,10},{10,1... | collective-permute-start | bytes 3145736 | tf_op jit(solution)/shard_map/ppermute | solution.py:60
  14.8 25.2 %collective-permute-done = bf16[512,1024]{1,0:T(8,128)(2,1)S(1)} collective-permute-done((bf16[512,1024]{1,0:T(8,128)(2,1)S(1)}, bf16[512,1024]{1,0:T(8,128)(2,1)S(1)}, u32[]{:S(2)}, u32[]{:S(2)}) %collective-permute-start) | collective-permute-done | bytes 1048608 | tf_op jit(solution)/shard_map/ppermute | solution.py:60
  40.0 0.0 collective-permute-start.1
  40.0 26.2 %collective-permute-done.1 = bf16[512,1024]{1,0:T(8,128)(2,1)} collective-permute-done((bf16[512,1024]{1,0:T(8,128)(2,1)S(1)}, bf16[512,1024]{1,0:T(8,128)(2,1)}, u32[]{:S(2)}, u32[]{:S(2)}) %collective-permute-start.1) | collective-permute-done | bytes 1048608 | tf_op jit(solution)/shard_map/ppermute | solution.py:60
  66.2 0.0 collective-permute-start.2
  66.2 0.0 copy-done
  66.2 2.8 convolution_bitcast_fusion
  69.0 1.4 copy.21
  70.4 0.0 copy-done.7
  70.4 0.1 iota_compare_fusion
  70.5 21.3 %collective-permute-done.2 = bf16[512,1024]{1,0:T(8,128)(2,1)} collective-permute-done((bf16[512,1024]{1,0:T(8,128)(2,1)}, bf16[512,1024]{1,0:T(8,128)(2,1)}, u32[]{:S(2)}, u32[]{:S(2)}) %collective-permute-start.2) | collective-permute-done | bytes 1048608 | tf_op jit(solution)/shard_map/ppermute | solution.py:60
  91.8 1.3 constant_dynamic-update-slice_fusion.7
  93.1 1.3 constant_dynamic-update-slice_fusion.6
  94.4 0.1 constant_dynamic-update-slice_fusion.5
  94.5 0.1 constant_dynamic-update-slice_fusion.4
  94.6 1.3 constant_dynamic-update-slice_fusion.3
  96.0 1.3 constant_dynamic-update-slice_fusion.2
  97.3 0.0 copy-start.6
  97.3 0.1 constant_dynamic-update-slice_fusion.1
  97.4 0.1 constant_dynamic-update-slice_fusion
  97.5 0.0 copy-start.3
  97.5 3.2 %copy-done.3 = bf16[512,8192]{1,0:T(8,128)(2,1)} copy-done((bf16[512,8192]{1,0:T(8,128)(2,1)}, bf16[512,8192]{1,0:T(8,128)(2,1)S(1)}, u32[]{:S(2)}) %copy-start.3) | copy-done | bytes 8388632
  100.7 0.9 fusion.3
  101.6 0.0 all-gather.9.cloned.1.call-done
  101.6 0.0 copy-done.6
  101.6 10.2 %fusion.27 = bf16[512,1024]{1,0:T(8,128)(2,1)} fusion(bf16[1,4096,1024]{2,1,0:T(8,128)(2,1)} %all-gather.9.cloned.1.call-done, f32[4096]{0:T(1024)S(1)} %bitcast.40, f32[512]{0:T(512)S(1)} %add_rsqrt_fusion, bf16[512,8192]{1,0:T(8,128)(2,1)} %copy-done.3, s32[]{:T(128)S(6)} %select_n.18), kind=kOutput, calls=%fused_computation.28 | convolution fusion | flops 4303880192 | bytes 13649924 | tf_op jit(solution)/shard_map/dot_general | solution.py:37
  111.8 2.9 reshape.48
  114.8 43.1 %all-gather.7.cloned.1.call-done = bf16[1,4096,2,1024]{3,1,2,0:T(8,128)(2,1)} async-done(((bf16[1,512,2,1024]{3,1,2,0:T(8,128)(2,1)}), bf16[1,4096,2,1024]{3,1,2,0:T(8,128)(2,1)}) %all-gather.7.cloned.1.call-update) | async-done | bytes 16777232 | tf_op jit(solution)/shard_map/all_gather | solution.py:82
  157.9 13.7 %convert_bitcast_fusion = bf16[2,512,1024]{2,1,0:T(8,128)(2,1)S(1)} fusion(bf16[1,4096,2,1024]{3,1,2,0:T(8,128)(2,1)} %all-gather.7.cloned.1.call-done, f32[4096]{0:T(1024)S(1)} %bitcast.41, f32[512]{0:T(512)S(1)} %add_rsqrt_fusion, bf16[512,8192]{1,0:T(8,128)(2,1)} %copy-done.3, s32[]{:T(128)S(6)} %select_n.18), kind=kOutput, calls=%fused_computation.23 | convolution fusion | flops 8599371776 | bytes 23087108 | tf_op jit(solution)/shard_map/td,dcf->ctf/dot_general | solution.py:38
  171.6 1.5 fusion.44
  173.1 4.0 %reshape.49 = bf16[4,128,16,64]{3,2,1,0:T(8,128)(2,1)} reshape(bf16[1,512,1024]{2,1,0:T(8,128)(2,1)} %get-tuple-element.6) | data formatting | bytes 2097152 | tf_op jit(solution)/shard_map/convert_element_type | solution.py:85
  177.2 4.0 %reshape.47 = bf16[4,128,16,64]{3,2,1,0:T(8,128)(2,1)} reshape(bf16[1,512,1024]{2,1,0:T(8,128)(2,1)} %get-tuple-element.5) | data formatting | bytes 2097152 | tf_op jit(solution)/shard_map/convert_element_type | solution.py:86
  181.2 0.0 copy-start.5
  181.2 3.2 %fusion.15 = f32[4,16,128,128]{2,3,1,0:T(8,128)S(1)} fusion(bf16[4,128,16,64]{3,2,1,0:T(8,128)(2,1)} %reshape.49, bf16[4,128,16,64]{3,2,1,0:T(8,128)(2,1)S(1)} %reshape.48), kind=kOutput, calls=%fused_computation.18 | convolution fusion | flops 134217728 | bytes 6291456 | tf_op jit(solution)/shard_map/cqhe,ckhe->chqk/dot_general | solution.py:91
  184.4 0.0 copy-done.5
  184.4 0.0 copy-start.4
  184.4 1.8 fusion.45
  186.2 0.0 copy-done.4
  186.3 0.8 fusion.33
  187.0 0.9 copy.24
  187.9 26.2 %all-gather.11.cloned.1.call-done = bf16[1,4096,1024]{2,1,0:T(8,128)(2,1)} async-done(((bf16[1,512,1024]{2,1,0:T(8,128)(2,1)}), bf16[1,4096,1024]{2,1,0:T(8,128)(2,1)}) %all-gather.11.cloned.1.call-update) | async-done | bytes 8388624 | tf_op jit(solution)/shard_map/all_gather | solution.py:103
  214.1 0.0 copy-start.1
  214.1 9.6 %fusion.10 = bf16[512,4096]{1,0:T(8,128)(2,1)} fusion(bf16[1,4096,1024]{2,1,0:T(8,128)(2,1)} %all-gather.11.cloned.1.call-done, bf16[128,8,4,128]{3,2,1,0:T(4,128)(2,1)S(1)} %bitcast.39), kind=kOutput, calls=%fused_computation.12 | convolution fusion | flops 4297064448 | bytes 13631488 | tf_op jit(solution)/shard_map/tf,df->td/dot_general | solution.py:100
  223.7 0.0 reduce-scatter.2.cloned.1.call-update
  223.7 77.0 %reduce-scatter.2.cloned.1.call-done = bf16[512,1024]{1,0:T(8,128)(2,1)} async-done(((bf16[512,4096]{1,0:T(8,128)(2,1)}), bf16[512,1024]{1,0:T(8,128)(2,1)}) %reduce-scatter.2.cloned.1.call-update) | async-done | bytes 1048592 | tf_op jit(solution)/shard_map/reduce_scatter | solution.py:106
  300.7 2.6 add_convert_fusion
  303.3 0.0 copy-done.1
  (1 shorter events, 0.0 us)
Async XLA Ops:
  6.5 59.7 %copy-start = (f32[1,32,16]{1,2,0:T(8,128)S(1)}, f32[1,32,16]{1,2,0:T(8,128)}, u32[]{:S(2)}) copy-start(f32[1,32,16]{1,2,0:T(8,128)} %param.13) | copy-start | bytes 6148
  6.5 5.2 %copy-start.2 = (bf16[512,1024]{1,0:T(8,128)(2,1)S(1)}, bf16[512,1024]{1,0:T(8,128)(2,1)}, u32[]{:S(2)}) copy-start(bf16[512,1024]{1,0:T(8,128)(2,1)} %param.8) | copy-start | bytes 3145732
  6.5 95.1 %all-gather.9.cloned.1.call-start = ((), (), s32[]{:S(2)}) async-start(), calls=%async_computation.3 | async-start | bytes 9437184 | tf_op jit(solution)/shard_map/all_gather | solution.py:81
  7.3 150.6 %all-gather.7.cloned.1.call-start = ((), (), s32[]{:S(2)}) async-start(), calls=%async_computation.2 | async-start | bytes 18874368 | tf_op jit(solution)/shard_map/all_gather | solution.py:82
  10.9 59.5 %copy-start.7 = (s32[4]{0:T(128)S(1)}, s32[4]{0:T(128)}, u32[]{:S(2)}) copy-start(s32[4]{0:T(128)} %param.14) | copy-start | bytes 52
  10.9 203.2 %all-gather.11.cloned.1.call-start = ((), (), s32[]{:S(2)}) async-start(), calls=%async_computation.4 | async-start | bytes 9437184 | tf_op jit(solution)/shard_map/all_gather | solution.py:103
  11.7 289.0 %reduce-scatter.2.cloned.1.call-start = ((), (), s32[]{:S(2)}) async-start(), calls=%async_computation.1 | async-start | bytes 5242880 | tf_op jit(solution)/shard_map/reduce_scatter | solution.py:106
  11.7 28.3 %collective-permute-start = (bf16[512,1024]{1,0:T(8,128)(2,1)S(1)}, bf16[512,1024]{1,0:T(8,128)(2,1)S(1)}, u32[]{:S(2)}, u32[]{:S(2)}) collective-permute-start(bf16[512,1024]{1,0:T(8,128)(2,1)S(1)} %copy-done.2), channel_id=1, source_target_pairs={{0,1},{1,2},{2,3},{3,0},{4,5},{5,6},{6,7},{7,4},{8,9},{9,10},{10,1... | collective-permute-start | bytes 3145736 | tf_op jit(solution)/shard_map/ppermute | solution.py:60
  40.0 26.2 %collective-permute-start.1 = (bf16[512,1024]{1,0:T(8,128)(2,1)S(1)}, bf16[512,1024]{1,0:T(8,128)(2,1)}, u32[]{:S(2)}, u32[]{:S(2)}) collective-permute-start(bf16[512,1024]{1,0:T(8,128)(2,1)S(1)} %collective-permute-done), channel_id=1, source_target_pairs={{0,1},{1,2},{2,3},{3,0},{4,5},{5,6},{6,7},{7,4},{8,9},{9,10},{10,1... | collective-permute-start | bytes 3145736 | tf_op jit(solution)/shard_map/ppermute | solution.py:60
  66.2 25.6 %collective-permute-start.2 = (bf16[512,1024]{1,0:T(8,128)(2,1)}, bf16[512,1024]{1,0:T(8,128)(2,1)}, u32[]{:S(2)}, u32[]{:S(2)}) collective-permute-start(bf16[512,1024]{1,0:T(8,128)(2,1)} %collective-permute-done.1), channel_id=1, source_target_pairs={{0,1},{1,2},{2,3},{3,0},{4,5},{5,6},{6,7},{7,4},{8,9},{9,10},{10,1... | collective-permute-start | bytes 3145736 | tf_op jit(solution)/shard_map/ppermute | solution.py:60
  97.3 4.3 %copy-start.6 = (f32[1,4096]{1,0:T(1,128)S(1)}, f32[1,4096]{1,0:T(1,128)}, u32[]{:S(2)}) copy-start(f32[1,4096]{1,0:T(1,128)} %param.9) | copy-start | bytes 49156
  97.5 3.2 %copy-start.3 = (bf16[512,8192]{1,0:T(8,128)(2,1)}, bf16[512,8192]{1,0:T(8,128)(2,1)S(1)}, u32[]{:S(2)}) copy-start(bf16[512,8192]{1,0:T(8,128)(2,1)S(1)} %constant_dynamic-update-slice_fusion) | copy-start | bytes 25165828
  181.2 3.3 %copy-start.5 = (f32[16,128,128]{1,2,0:T(8,128)S(1)}, f32[16,128,128]{1,2,0:T(8,128)}, u32[]{:S(2)}) copy-start(f32[16,128,128]{1,2,0:T(8,128)} %copy.21) | copy-start | bytes 3145732
  184.4 1.8 copy-start.4
  214.1 89.2 %copy-start.1 = (f32[1,32,16]{1,2,0:T(8,128)S(1)}, f32[1,32,16]{1,2,0:T(8,128)}, u32[]{:S(2)}) copy-start(f32[1,32,16]{1,2,0:T(8,128)} %param.13) | copy-start | bytes 6148
Sparse Core Ops, SparseCore 0:
  9.2 56.9 all-gather.8
  68.1 89.7 all-gather.6
  159.8 54.2 all-gather.10
  223.8 76.7 reduce-scatter.1
